TPU v7x, 512 devices: a whole 4x8x8 slice. The times are simulated.
512 devices in a mesh: region: 32 (over x, y), shard: 16 (over z, core).
Axes of the slice: x: 4, y: 8, z: 8, core: 2. Of those that a mesh axis runs over, the one named last changes fastest.
Arguments:
- planes: bfloat16 [4, 16384, 512], P(None, ('region', 'shard')), may hold values from -6 to 6
- sed_weights: float32 [6, 4], replicated, may hold values from 0.1 to 2
- psf_taps: float32 [2, 6, 3, 25], replicated, may hold values from 0.004 to 0.08
- resample_rows: bfloat16 [16384, 128, 128], P(('region', 'shard')), may hold values from -0.5 to 0.5
- resample_cols: bfloat16 [16384, 128, 256], P(('region', 'shard')), may hold values from -0.375 to 0.375
- observed: bfloat16 [16384, 128, 128], P(('region', 'shard')), may hold values from -6 to 6
- exposure_meta: int32 [3, 16384], P(None, 'region'), may hold values from 0 to 15, as said below
- slot_counts: int32 [32, 16], P('region'), may hold values from 8 to 32, as said below
Outputs:
- plane_grad: float32 [4, 16384, 512], P(None, ('region', 'shard'))
Inputs may be any that keep to these rules, and one draw needn't show every extreme that they name: `exposure_meta`: row 0 is a row tile of the exposure's region, 0 to 15; row 1 a column tile, 0 to 1; row 2 a band, 0 to 5. `slot_counts`: the live slots of a device are its first ones. In every region one device has all 32 slots live, the others between 8 and 16.
All inputs are finite; a program needn't handle non-finite values.
Results may differ from a plain program's by a relative error of at most 0.003.
Values may be sent and summed in bfloat16 or wider, within the bound.
A program may use at most 64 MiB of HBM per device.

v0:
```python
import jax
import jax.numpy as jnp
from jax import lax
from jax.sharding import PartitionSpec as P

GROUP = 4


def passed_along(block, axis, distance):
    devices = range(lax.axis_size(axis))
    route = [(i - distance, i) for i in devices if i - distance in devices]
    return lax.ppermute(block, axis, route)


def band_tables(taps, width):
    tap_count = taps.shape[-1]
    offset = (
        jnp.arange(width, dtype=jnp.int32)[:, None]
        - jnp.arange(width, dtype=jnp.int32)[None, :]
        + tap_count // 2
    )
    selector = (offset[None, :, :] == jnp.arange(tap_count, dtype=jnp.int32)[:, None, None]).astype(
        jnp.float32
    )
    return jnp.einsum("btk,kij->btij", taps, selector, precision=lax.Precision.HIGHEST).astype(
        jnp.bfloat16
    )


def local(
    planes,
    sed_weights,
    psf_taps,
    resample_rows,
    resample_cols,
    observed,
    exposure_meta,
    slot_counts,
):
    shard_count = lax.axis_size("shard")
    my_index = lax.axis_index("shard")
    channel_count, tile_rows, col_total = planes.shape
    slot_count, out_rows, win_rows = resample_rows.shape
    win_cols = resample_cols.shape[2]
    region_rows = tile_rows * shard_count
    rim_rows = win_rows - tile_rows
    gathered = lax.all_gather(planes, "shard", axis=1, tiled=True)
    next_part = passed_along(gathered[:, :rim_rows], "region", -1)
    extended = jnp.concatenate([gathered, next_part], axis=1)
    rows_tab = band_tables(psf_taps[0], win_rows)
    cols_tab = band_tables(psf_taps[1], win_cols)
    live_counts = slot_counts[0]
    device_ids = jnp.arange(shard_count, dtype=jnp.int32)
    position = jnp.arange(slot_count, dtype=jnp.int32)
    my_count = jnp.sum(jnp.where(device_ids == my_index, live_counts, 0))
    row_maps, col_maps, pixel_sets = (resample_rows, resample_cols, observed)
    is_live = position < my_count
    region_slot = my_index * slot_count + position
    meta_total = exposure_meta.shape[1]
    matches = (jnp.arange(meta_total, dtype=jnp.int32)[:, None] == region_slot[None, :]).astype(
        jnp.int32
    )
    meta_sel = jnp.dot(exposure_meta, matches)
    live_rank = jnp.cumsum(is_live.astype(jnp.int32)) - 1
    picks = jnp.logical_and(is_live[:, None], live_rank[:, None] == position[None, :])
    live_order = jnp.sum(jnp.where(picks, position[:, None], 0), axis=0)
    live_total = jnp.sum(is_live.astype(jnp.int32))
    turn_total = (live_total + GROUP - 1) // GROUP

    def cut_window(start_row, start_col):
        return lax.dynamic_slice(
            extended, (jnp.int32(0), start_row, start_col), (channel_count, win_rows, win_cols)
        )

    def visit(turn_index, gradient):
        ranks = turn_index * GROUP + jnp.arange(GROUP, dtype=jnp.int32)
        usable = ranks < live_total
        chosen = jnp.take(live_order, jnp.minimum(ranks, slot_count - 1))
        row_start = jnp.take(meta_sel[0], chosen) * tile_rows
        col_start = jnp.take(meta_sel[1], chosen) * win_cols
        band_of = jnp.take(meta_sel[2], chosen)
        windows = jax.vmap(cut_window)(row_start, col_start)
        sed_sel = jnp.take(sed_weights, band_of, axis=0)
        py_mat = jnp.take(rows_tab, band_of, axis=0)
        px_mat = jnp.take(cols_tab, band_of, axis=0)
        ry_mat = jnp.take(row_maps, chosen, axis=0)
        rx_mat = jnp.take(col_maps, chosen, axis=0)
        pixels = jnp.take(pixel_sets, chosen, axis=0)
        mixed = jnp.sum(sed_sel[:, :, None, None] * windows.astype(jnp.float32), axis=1).astype(
            jnp.bfloat16
        )
        smeared = jnp.einsum(
            "gtiy,gyx->gtix", py_mat, mixed, preferred_element_type=jnp.float32
        ).astype(jnp.bfloat16)
        blurred = jnp.einsum(
            "gtix,gtjx->gij", smeared, px_mat, preferred_element_type=jnp.float32
        ).astype(jnp.bfloat16)
        sampled = jnp.einsum(
            "goy,gyx->gox", ry_mat, blurred, preferred_element_type=jnp.float32
        ).astype(jnp.bfloat16)
        model = jnp.einsum("gox,gpx->gop", sampled, rx_mat, preferred_element_type=jnp.float32)
        misfit = (model - pixels.astype(jnp.float32)).astype(jnp.bfloat16)
        back_rows = jnp.einsum(
            "goy,gop->gyp", ry_mat, misfit, preferred_element_type=jnp.float32
        ).astype(jnp.bfloat16)
        back = jnp.einsum(
            "gyp,gpx->gyx", back_rows, rx_mat, preferred_element_type=jnp.float32
        ).astype(jnp.bfloat16)
        unsmeared = jnp.einsum(
            "gtiy,gix->gtyx", py_mat, back, preferred_element_type=jnp.float32
        ).astype(jnp.bfloat16)
        window_grad = jnp.einsum(
            "gtyj,gtjx->gyx", unsmeared, px_mat, preferred_element_type=jnp.float32
        )
        contrib = sed_sel[:, :, None, None] * window_grad[:, None]
        for member in range(GROUP):
            corner = (jnp.int32(0), row_start[member], col_start[member])
            current = lax.dynamic_slice(gradient, corner, (channel_count, win_rows, win_cols))
            added = jnp.where(usable[member], contrib[member], 0.0)
            gradient = lax.dynamic_update_slice(gradient, current + added, corner)
        return gradient

    start = jnp.zeros((channel_count, region_rows + rim_rows, col_total), jnp.float32)
    gradient = lax.fori_loop(0, turn_total, visit, start)
    incoming = passed_along(gradient[:, region_rows:], "region", 1)
    own_rows = gradient[:, :region_rows].at[:, :rim_rows].add(incoming)
    return lax.psum_scatter(own_rows, "shard", scatter_dimension=1, tiled=True)


def solution(mesh):
    placed = (
        P(None, ("region", "shard"), None),
        P(),
        P(),
        P(("region", "shard"), None, None),
        P(("region", "shard"), None, None),
        P(("region", "shard"), None, None),
        P(None, "region"),
        P("region", None),
    )
    return jax.shard_map(
        local,
        mesh=mesh,
        in_specs=placed,
        out_specs=P(None, ("region", "shard"), None),
        check_vma=False,
    )
```

profile of v0, /device:TPU:2, one launch (start us, length us, event | category | flops | bytes accessed | tf_op | source)
XLA Modules:
  0.0 797.5 jit_solution(13557028132865648355)
XLA Ops:
  12.8 3.9 convert_bitcast_fusion
  16.7 40.7 %all-gather.2.cloned.1.call-done = bf16[4,512,512]{2,1,0:T(8,128)(2,1)} async-done(((bf16[4,32,512]{2,1,0:T(8,128)(2,1)}), bf16[4,512,512]{2,1,0:T(8,128)(2,1)}) %all-gather.2.cloned.1.call-update) | async-done | bytes 2097168 | tf_op jit(solution)/shard_map/all_gather | solution.py:47
  59.2 4.7 collective-permute-start
  66.0 2.1 copy.27
  68.1 2.0 copy.28
  70.4 2.5 collective-permute-done
  73.0 3.4 pad_maximum_fusion
  76.3 2.8 broadcast_in_dim.101
  79.2 234.0 %while.14 = (s32[]{:T(128)}, f32[4,608,512]{2,1,0:T(8,128)}, s32[]{:T(128)}, s32[3,32]{1,0:T(4,128)S(1)}, s32[32]{0:T(128)S(1)}, /*index=5*/s32[]{:T(128)}, f32[...) while((s32[]{:T(128)}, f32[4,608,512]{2,1,0:T(8,128)}, ...), condition=%wide.region_6.9_spmd, body=%wide.region_4.8_spmd.sunk | while | flops 728304896 | bytes 28457620 | solution.py:124
  104.1 2.2 gather_fusion.8
  106.9 12.8 %while.15 = (s32[]{:T(128)}, bf16[4,608,512]{2,1,0:T(8,128)(2,1)}, s32[4,3]{1,0:T(4,128)S(1)}, bf16[4,4,128,256]{3,2,1,0:T(8,128)(2,1)S(1)}, s32[]{:T(128)}) while((s32[]{:T(128)}, bf16[4,608,512]{2,1,0:T(8,128)(2,1)}, s32[4,3]{1,0:T(4,128)S(1)}, bf16[4,4,128,256]{3,2,1,0:T(8,128)(2,1)S(1)}, s32[]{:T(128)}) %tuple.81), condition=%wide.while_cond.1, body=%wide.while_body.1.sunk | while | flops 2 | bytes 524413 | solution.py:71
  107.6 2.5 bitcast_dynamic-update-slice_fusion.2
  110.8 2.5 bitcast_dynamic-update-slice_fusion.2
  114.0 2.5 bitcast_dynamic-update-slice_fusion.2
  117.2 2.5 bitcast_dynamic-update-slice_fusion.2
  120.0 2.3 gather_fusion.2
  129.6 5.2 dynamic_update_slice.16
  136.8 5.9 dynamic_update_slice.17
  144.6 5.9 dynamic_update_slice.18
  152.5 5.3 dynamic_update_slice.19
  182.6 2.2 gather_fusion.8
  185.5 12.8 %while.15 = (s32[]{:T(128)}, bf16[4,608,512]{2,1,0:T(8,128)(2,1)}, s32[4,3]{1,0:T(4,128)S(1)}, bf16[4,4,128,256]{3,2,1,0:T(8,128)(2,1)S(1)}, s32[]{:T(128)}) while((s32[]{:T(128)}, bf16[4,608,512]{2,1,0:T(8,128)(2,1)}, s32[4,3]{1,0:T(4,128)S(1)}, bf16[4,4,128,256]{3,2,1,0:T(8,128)(2,1)S(1)}, s32[]{:T(128)}) %tuple.81), condition=%wide.while_cond.1, body=%wide.while_body.1.sunk | while | flops 2 | bytes 524413 | solution.py:71
  186.2 2.5 bitcast_dynamic-update-slice_fusion.2
  189.4 2.5 bitcast_dynamic-update-slice_fusion.2
  192.5 2.5 bitcast_dynamic-update-slice_fusion.2
  195.7 2.5 bitcast_dynamic-update-slice_fusion.2
  198.5 2.3 gather_fusion.2
  208.1 5.3 dynamic_update_slice.16
  215.3 5.3 dynamic_update_slice.17
  222.4 5.2 dynamic_update_slice.18
  227.7 2.1 fusion.93
  229.7 5.9 dynamic_update_slice.19
  260.5 2.2 gather_fusion.8
  263.3 12.8 %while.15 = (s32[]{:T(128)}, bf16[4,608,512]{2,1,0:T(8,128)(2,1)}, s32[4,3]{1,0:T(4,128)S(1)}, bf16[4,4,128,256]{3,2,1,0:T(8,128)(2,1)S(1)}, s32[]{:T(128)}) while((s32[]{:T(128)}, bf16[4,608,512]{2,1,0:T(8,128)(2,1)}, s32[4,3]{1,0:T(4,128)S(1)}, bf16[4,4,128,256]{3,2,1,0:T(8,128)(2,1)S(1)}, s32[]{:T(128)}) %tuple.81), condition=%wide.while_cond.1, body=%wide.while_body.1.sunk | while | flops 2 | bytes 524413 | solution.py:71
  264.1 2.5 bitcast_dynamic-update-slice_fusion.2
  267.2 2.5 bitcast_dynamic-update-slice_fusion.2
  270.5 2.5 bitcast_dynamic-update-slice_fusion.2
  273.6 2.5 bitcast_dynamic-update-slice_fusion.2
  276.4 2.3 gather_fusion.2
  286.0 5.3 dynamic_update_slice.16
  293.3 5.9 dynamic_update_slice.17
  301.0 5.0 dynamic_update_slice.18
  308.0 5.2 dynamic_update_slice.19
  314.4 3.3 collective-permute-start.1
  317.7 4.7 slice.100
  322.4 88.7 %collective-permute-done.1 = f32[4,96,512]{2,1,0:T(8,128)S(1)} collective-permute-done((f32[4,96,512]{2,1,0:T(8,128)S(1)}, f32[4,96,512]{2,1,0:T(8,128)S(1)}, u32[]{:S(2)}, u32[]{:S(2)}) %collective-permute-start.1) | collective-permute-done | bytes 786464 | tf_op jit(solution)/shard_map/ppermute | solution.py:12
  411.1 2.2 add_dynamic-update-slice_fusion
  413.4 377.3 %reduce-scatter.2.cloned.1.call-done = f32[4,32,512]{2,1,0:T(8,128)} async-done(((f32[4,512,512]{2,1,0:T(8,128)}), f32[4,32,512]{2,1,0:T(8,128)}) %reduce-scatter.2.cloned.1.call-update) | async-done | bytes 262160 | tf_op jit(solution)/shard_map/reduce_scatter | solution.py:127
  (157 shorter events, 88.1 us)
Async XLA Ops:
  6.5 63.7 %copy-start = (s32[3,512]{1,0:T(4,128)S(1)}, s32[3,512]{1,0:T(4,128)}, u32[]{:S(2)}) copy-start(s32[3,512]{1,0:T(4,128)} %param.22) | copy-start | bytes 18436
  6.5 50.8 %all-gather.2.cloned.1.call-start = ((), (), s32[]{:S(2)}) async-start(), calls=%async_computation.1 | async-start | bytes 2228224 | tf_op jit(solution)/shard_map/all_gather | solution.py:47
  7.3 783.4 %reduce-scatter.2.cloned.1.call-start = ((), (), s32[]{:S(2)}) async-start(), calls=%async_computation.2 | async-start | bytes 4456448 | tf_op jit(solution)/shard_map/reduce_scatter | solution.py:127
  12.8 53.1 %copy-start.3 = (f32[6,4]{0,1:T(4,128)S(1)}, f32[6,4]{0,1:T(4,128)}, u32[]{:S(2)}) copy-start(f32[6,4]{0,1:T(4,128)} %param.17) | copy-start | bytes 292
  59.2 13.8 %collective-permute-start = (bf16[4,96,512]{2,1,0:T(8,128)(2,1)}, bf16[4,96,512]{2,1,0:T(8,128)(2,1)}, u32[]{:S(2)}, u32[]{:S(2)}) collective-permute-start(bf16[4,96,512]{2,1,0:T(8,128)(2,1)} %slice.142), channel_id=1, source_target_pairs={{16,0},{32,16},{48,32},{64,48},{80,64},{96,80},{112,96},{128,112},... | collective-permute-start | bytes 1179656 | tf_op jit(solution)/shard_map/ppermute | solution.py:12
  76.3 2.8 copy-start.1
  106.9 15.5 %copy-start.2 = (bf16[4,3,128,128]{3,2,1,0:T(8,128)(2,1)}, bf16[4,3,128,128]{3,2,1,0:T(8,128)(2,1)S(1)}, u32[]{:S(2)}) copy-start(bf16[4,3,128,128]{3,2,1,0:T(8,128)(2,1)S(1)} %gather_fusion.6) | copy-start | bytes 1179652 | tf_op jit(solution)/shard_map/while
  185.4 15.4 %copy-start.2 = (bf16[4,3,128,128]{3,2,1,0:T(8,128)(2,1)}, bf16[4,3,128,128]{3,2,1,0:T(8,128)(2,1)S(1)}, u32[]{:S(2)}) copy-start(bf16[4,3,128,128]{3,2,1,0:T(8,128)(2,1)S(1)} %gather_fusion.6) | copy-start | bytes 1179652 | tf_op jit(solution)/shard_map/while
  263.3 15.4 %copy-start.2 = (bf16[4,3,128,128]{3,2,1,0:T(8,128)(2,1)}, bf16[4,3,128,128]{3,2,1,0:T(8,128)(2,1)S(1)}, u32[]{:S(2)}) copy-start(bf16[4,3,128,128]{3,2,1,0:T(8,128)(2,1)S(1)} %gather_fusion.6) | copy-start | bytes 1179652 | tf_op jit(solution)/shard_map/while
  314.4 96.7 %collective-permute-start.1 = (f32[4,96,512]{2,1,0:T(8,128)S(1)}, f32[4,96,512]{2,1,0:T(8,128)S(1)}, u32[]{:S(2)}, u32[]{:S(2)}) collective-permute-start(f32[4,96,512]{2,1,0:T(8,128)S(1)} %slice.102), channel_id=1, source_target_pairs={{0,16},{16,32},{32,48},{48,64},{64,80},{80,96},{96,112},{112,128},... | collective-permute-start | bytes 2359304 | tf_op jit(solution)/shard_map/ppermute | solution.py:12
Sparse Core Ops, SparseCore 0:
  9.5 47.8 all-gather.1
  413.5 377.0 reduce-scatter.1
where the time goes:
time: 808 us; the launch traced here: 797 us
  waiting for transfers between devices  510 us (63%)
  local copies, waits for them, and re-layouts  160 us (20%)
  loops' own time  46.3 us (6%)
  other arithmetic  37.2 us (5%)
  matrix products  21.3 us (3%)
  between operations  14.2 us (2%)
  starting transfers between devices  8.1 us (1%)
    reduce_scatter x1, waiting for transfers between devices, local(): return lax.psum_scatter(own_rows, 'shard', scatter_dimension=1, tiled=True)  377 us
    ppermute x2, waiting for transfers between devices, passed_along(): return lax.ppermute(block, axis, route)  91.3 us
    dynamic_update_slice x12, local copies, waits for them, and re-layouts, visit(): gradient = lax.dynamic_update_slice(gradient, current + added, corner)  65.2 us
    another operation x1, loops' own time, local(): gradient = lax.fori_loop(0, turn_total, visit, start)  45.9 us
    all_gather x1, waiting for transfers between devices, local(): gathered = lax.all_gather(planes, 'shard', axis=1, tiled=True)  40.7 us
    gather x36, local copies, waits for them, and re-layouts  38.1 us
    add x12, other arithmetic, visit(): gradient = lax.dynamic_update_slice(gradient, current + added, corner)  23 us
  transfers between devices with their start and end apart: 4, of which 4 were waited for; matrix products, arithmetic and copies ran while one was open for 2% of the time, Pallas kernels for 0%

commit v1 on v0

v1 whole, which is shorter than its diff:
```python
import functools

import jax
import jax.numpy as jnp
from jax import lax
from jax.experimental import pallas as pl
from jax.experimental.pallas import tpu as pltpu
from jax.sharding import PartitionSpec as P

F32 = jnp.float32
BF16 = jnp.bfloat16
GROUP = 4


def passed_along(block, axis, distance):
    devices = range(lax.axis_size(axis))
    route = [(i - distance, i) for i in devices if i - distance in devices]
    return lax.ppermute(block, axis, route)


def dot(a, b, ca=1, cb=0):
    return lax.dot_general(a, b, (((ca,), (cb,)), ((), ())), preferred_element_type=F32)


def toeplitz(base, size):
    wide = jnp.broadcast_to(base, (size, base.shape[-1]))
    return pltpu.roll(wide, 0, 1, stride=1, stride_axis=0)[:, :size].astype(BF16)


def bases(taps, size):
    count = taps.shape[-1]
    half, length = count // 2, size + 128
    flat = taps.reshape(-1, 1, count)

    def place(v):
        gap = jnp.zeros(v.shape[:-1] + (length - count,), F32)
        return jnp.concatenate([v[..., half:], gap, v[..., :half]], axis=-1)

    return jnp.stack([place(flat[..., ::-1]), place(flat)], axis=1).reshape(-1, 1, length)


def grad_kernel(
    bands, terms, tile,
    counts, meta, sed, rbase, cbase, planes, ry_hbm, rx_hbm, ob_hbm,
    out,
    ry, rx, ob, rows_tab, rows_tab_t, cols_tab, cols_tab_t, sems,
):
    me = lax.axis_index("shard")
    slots, _, wy = ry.shape
    wx = rx.shape[2]
    comps = planes.shape[0]
    count = counts[0, me]
    turns = (count + GROUP - 1) // GROUP
    pairs = ((ry_hbm, ry), (rx_hbm, rx), (ob_hbm, ob))

    def copies(turn):
        part = pl.ds(turn * GROUP, GROUP)
        return [
            pltpu.make_async_copy(far.at[part], near.at[part], sems.at[j, turn])
            for j, (far, near) in enumerate(pairs)
        ]

    @pl.loop(0, turns)
    def _(turn):
        for copy in copies(turn):
            copy.start()

    @pl.loop(0, bands)
    def _(band):
        for t in range(terms):
            for d in range(2):
                at = (band * terms + t) * 2 + d
                (rows_tab, rows_tab_t)[d][band, :, t * wy : (t + 1) * wy] = toeplitz(rbase[at], wy)
                (cols_tab, cols_tab_t)[d][band, :, t * wx : (t + 1) * wx] = toeplitz(cbase[at], wx)

    out[...] = jnp.zeros_like(out)

    def stack(a, width):
        return jnp.concatenate([a[:, t * width : (t + 1) * width] for t in range(terms)], axis=0)

    @pl.loop(0, turns)
    def _(turn):
        for copy in copies(turn):
            copy.wait()
        members = range(GROUP)
        slot = [turn * GROUP + g for g in members]
        at = [me * slots + e for e in slot]
        band = [meta[2, p] for p in at]
        window = [
            (
                pl.ds(pl.multiple_of(meta[0, p] * tile, tile), wy),
                pl.ds(pl.multiple_of(meta[1, p] * wx, wx), wx),
            )
            for p in at
        ]
        mixed = [
            sum(sed[band[g], k] * planes[(k,) + window[g]].astype(F32) for k in range(comps)).astype(BF16)
            for g in members
        ]
        smeared = [dot(mixed[g], cols_tab_t[band[g]]).astype(BF16) for g in members]
        blurred = [dot(rows_tab[band[g]], stack(smeared[g], wx)).astype(BF16) for g in members]
        sampled = [dot(ry[slot[g]], blurred[g]).astype(BF16) for g in members]
        misfit = [
            (dot(sampled[g], rx[slot[g]], 1, 1) - ob[slot[g]].astype(F32)).astype(BF16) for g in members
        ]
        back_rows = [dot(ry[slot[g]], misfit[g], 0, 0).astype(BF16) for g in members]
        back = [dot(back_rows[g], rx[slot[g]]).astype(BF16) for g in members]
        unsmeared = [dot(back[g], cols_tab[band[g]]).astype(BF16) for g in members]
        window_grad = [dot(rows_tab_t[band[g]], stack(unsmeared[g], wx)) for g in members]
        for g in members:
            usable = slot[g] < count
            for k in range(comps):
                weight = jnp.where(usable, sed[band[g], k], 0.0)
                part = (k,) + window[g]
                out[part] = out[part] + weight * window_grad[g]


def gradient_of(planes, sed, taps, ry, rx, ob, meta, counts, tile):
    slots, _, wy = ry.shape
    wx = rx.shape[2]
    bands, terms = taps.shape[1:3]
    scalars = pl.BlockSpec(memory_space=pltpu.SMEM)
    near = pl.BlockSpec(memory_space=pltpu.VMEM)
    far = pl.BlockSpec(memory_space=pl.ANY)
    tables = [(bands, wy, terms * wy)] * 2 + [(bands, wx, terms * wx)] * 2
    return pl.pallas_call(
        functools.partial(grad_kernel, bands, terms, tile),
        out_shape=jax.ShapeDtypeStruct(planes.shape, F32),
        in_specs=[scalars] * 3 + [near] * 3 + [far] * 3,
        out_specs=near,
        scratch_shapes=[pltpu.VMEM(a.shape, a.dtype) for a in (ry, rx, ob)]
        + [pltpu.VMEM(shape, BF16) for shape in tables]
        + [pltpu.SemaphoreType.DMA((3, slots // GROUP))],
        compiler_params=pltpu.CompilerParams(vmem_limit_bytes=56 << 20),
    )(counts, meta, sed, bases(taps[0], wy), bases(taps[1], wx), planes, ry, rx, ob)


def local(planes, sed, taps, ry, rx, ob, meta, counts):
    tile = planes.shape[1]
    region_rows = tile * lax.axis_size("shard")
    rim_rows = ry.shape[2] - tile
    gathered = lax.all_gather(planes, "shard", axis=1, tiled=True)
    next_part = passed_along(gathered[:, :rim_rows], "region", -1)
    extended = jnp.concatenate([gathered, next_part], axis=1)
    gradient = gradient_of(extended, sed, taps, ry, rx, ob, meta, counts, tile)
    incoming = passed_along(gradient[:, region_rows:], "region", 1)
    own_rows = gradient[:, :region_rows].at[:, :rim_rows].add(incoming)
    return lax.psum_scatter(own_rows, "shard", scatter_dimension=1, tiled=True)


def solution(mesh):
    shards = P(("region", "shard"), None, None)
    placed = (P(None, ("region", "shard"), None), P(), P(), shards, shards, shards)
    placed += (P(None, "region"), P("region", None))
    return jax.shard_map(
        local,
        mesh=mesh,
        in_specs=placed,
        out_specs=P(None, ("region", "shard"), None),
        check_vma=False,
    )
```

time: 808 us -> 185 us (0.23); the launches traced: 797 us -> 185 us
  waiting for transfers between devices: 510 us -> 127 us
  local copies, waits for them, and re-layouts: 160 us -> 9.95 us
  loops' own time: 46.3 us -> 0 us
  other arithmetic: 37.2 us -> 6.98 us
  matrix products: 21.3 us -> 0 us
  Pallas kernels: 0 us -> 11.1 us
    reduce_scatter x1, waiting for transfers between devices: 377 us -> 61.5 us  [local(): return lax.psum_scatter(own_rows, 'shard', scatter_dimension=1, tiled=True)]
    ppermute x2, waiting for transfers between devices: 91.3 us -> 16.6 us  [passed_along(): return lax.ppermute(block, axis, route)]
    gather x66 -> x0, local copies, waits for them, and re-layouts: 73.5 us -> none
    dynamic_update_slice x12 -> x0, local copies, waits for them, and re-layouts: 65.2 us -> none  [visit(): gradient = lax.dynamic_update_slice(gradient, current + added, corner)]
    another operation x4 -> x0, loops' own time: 46.3 us -> none  [the longest x1 45.9 us: local(): gradient = lax.fori_loop(0, turn_total, visit, start)]
    add x15 -> x0, other arithmetic: 23.1 us -> none  [the longest x12 23 us: visit(): gradient = lax.dynamic_update_slice(gradient, current + added, corner)]
    dot_general x15 -> x0, matrix products: 21.3 us -> none  [the longest x2 5.73 us: band_tables(): jnp.einsum('btk,kij->btij', taps, selector, precision=lax.Precision.HIGHEST)]
    pallas_call x0 -> x1, Pallas kernels: none -> 11.1 us  [gradient_of(): pl.pallas_call(functools.partial(grad_kernel, bands, terms, tile), out_sh...]
  transfers between devices with their start and end apart: 4 -> 4, of which waited for: 4 -> 4; matrix products, arithmetic and copies ran while one was open for 2% -> 5% of each run, Pallas kernels for 0% -> 0%
where the time goes in v1:
time: 185 us
  waiting for transfers between devices  127 us (69%)
  starting transfers between devices  15.8 us (9%)
  between operations  13.5 us (7%)
  Pallas kernels  11.1 us (6%)
  local copies, waits for them, and re-layouts  9.95 us (5%)
  other arithmetic  6.98 us (4%)
    reduce_scatter x1, waiting for transfers between devices, local(): return lax.psum_scatter(own_rows, 'shard', scatter_dimension=1, tiled=True)  61.5 us
    all_gather x1, waiting for transfers between devices, local(): gathered = lax.all_gather(planes, 'shard', axis=1, tiled=True)  48.5 us
    ppermute x2, waiting for transfers between devices, passed_along(): return lax.ppermute(block, axis, route)  16.6 us
    ppermute x2, starting transfers between devices, passed_along(): return lax.ppermute(block, axis, route)  15.8 us
    pallas_call x1, Pallas kernels, gradient_of(): pl.pallas_call(functools.partial(grad_kernel, bands, terms, tile), out_sh...  11.1 us
    slice x1, local copies, waits for them, and re-layouts, local(): own_rows = gradient[:, :region_rows].at[:, :rim_rows].add(incoming)  4.63 us
  transfers between devices with their start and end apart: 4, of which 4 were waited for; matrix products, arithmetic and copies ran while one was open for 5% of the time, Pallas kernels for 0%

profile of v1, /device:TPU:2, one launch (start us, length us, event | category | flops | bytes accessed | tf_op | source)
XLA Modules:
  0.0 184.6 jit_solution(18104891185588586813)
XLA Ops:
  6.5 0.0 all-gather.2.cloned.1.call-start
  6.5 0.7 all-gather.2.cloned.1.call-update
  7.3 0.0 reduce-scatter.2.cloned.1.call-start
  7.3 0.8 fusion.1
  8.1 0.1 fusion.5
  8.2 0.1 slice.80
  8.3 0.1 fusion.4
  8.4 0.1 slice.78
  8.5 0.1 pad.18.clone
  8.6 0.1 fusion.3
  8.7 0.1 fusion.2
  8.8 0.1 maximum_bitcast_fusion.2
  8.9 48.5 %all-gather.2.cloned.1.call-done = bf16[4,512,512]{2,1,0:T(8,128)(2,1)} async-done(((bf16[4,32,512]{2,1,0:T(8,128)(2,1)}), bf16[4,512,512]{2,1,0:T(8,128)(2,1)}) %all-gather.2.cloned.1.call-update) | async-done | bytes 2097168 | tf_op jit(solution)/shard_map/all_gather | solution.py:142
  57.4 1.0 slice.102
  58.4 4.7 %collective-permute-start = (bf16[4,96,512]{2,1,0:T(8,128)(2,1)S(1)}, bf16[4,96,512]{2,1,0:T(8,128)(2,1)S(1)}, u32[]{:S(2)}, u32[]{:S(2)}) collective-permute-start(bf16[4,96,512]{2,1,0:T(8,128)(2,1)S(1)} %slice.102), channel_id=1, source_target_pairs={{16,0},{32,16},{48,32},{64,48},{80,64},{96,80},{112,96},{128,112},... | collective-permute-start | bytes 1179656 | tf_op jit(solution)/shard_map/ppermute | solution.py:18
  63.1 0.6 pad_maximum_fusion.2
  63.8 0.1 pad.10.clone
  63.9 1.4 copy.11.sed
  65.2 0.1 slice.87
  65.3 0.1 slice.85
  65.5 0.1 maximum_bitcast_fusion
  65.6 0.7 pad_maximum_fusion.1
  66.3 5.7 %collective-permute-done = bf16[4,96,512]{2,1,0:T(8,128)(2,1)S(1)} collective-permute-done((bf16[4,96,512]{2,1,0:T(8,128)(2,1)S(1)}, bf16[4,96,512]{2,1,0:T(8,128)(2,1)S(1)}, u32[]{:S(2)}, u32[]{:S(2)}) %collective-permute-start) | collective-permute-done | bytes 393248 | tf_op jit(solution)/shard_map/ppermute | solution.py:18
  71.9 3.2 %pad_maximum_fusion.planes = bf16[4,608,512]{2,1,0:T(8,128)(2,1)} fusion(bf16[4,96,512]{2,1,0:T(8,128)(2,1)S(1)} %collective-permute-done, bf16[4,512,512]{2,1,0:T(8,128)(2,1)} %all-gather.2.cloned.1.call-done), kind=kLoop, calls=%fused_computation | loop fusion | flops 4980736 | bytes 4980736 | tf_op jit(solution)/shard_map/concatenate | solution.py:144
  75.2 11.1 %shard_map.82 = f32[4,608,512]{2,1,0:T(8,128)} custom-call(s32[1,16]{1,0:T(1,128)} %counts.1, s32[3,512]{1,0:T(4,128)} %meta.1, f32[6,4]{1,0:T(8,128)} %copy.11.sed, f32[36,1,256]{2,1,0:T(1,128)} %bitcast.21, f32[36,1,384]{2,1,0:T(1,128)} %bitcast.20, bf16[4,608,512]{2,1,0:T(8,128)(2,1)} %pad_maximum_fusion.planes, bf16[32,128,128]{2,1,0:T(8,128)(2,1)} %ry_hbm.1, ...), custom_call_target="tpu_custom_call" | custom-call | tf_op jit(solution)/shard_map/pallas_call | solution.py:126
  86.3 1.2 slice.105
  87.5 11.0 %collective-permute-start.1 = (f32[4,96,512]{2,1,0:T(8,128)S(1)}, f32[4,96,512]{2,1,0:T(8,128)S(1)}, u32[]{:S(2)}, u32[]{:S(2)}) collective-permute-start(f32[4,96,512]{2,1,0:T(8,128)S(1)} %slice.105), channel_id=1, source_target_pairs={{0,16},{16,32},{32,48},{48,64},{64,80},{80,96},{96,112},{112,128},... | collective-permute-start | bytes 2359304 | tf_op jit(solution)/shard_map/ppermute | solution.py:18
  98.5 4.6 %slice.103 = f32[4,512,512]{2,1,0:T(8,128)} slice(f32[4,608,512]{2,1,0:T(8,128)} %shard_map.82), slice={[0:4], [0:512], [0:512]} | slice | bytes 8388608 | tf_op jit(solution)/shard_map/slice | solution.py:147
  103.2 10.9 %collective-permute-done.1 = f32[4,96,512]{2,1,0:T(8,128)S(1)} collective-permute-done((f32[4,96,512]{2,1,0:T(8,128)S(1)}, f32[4,96,512]{2,1,0:T(8,128)S(1)}, u32[]{:S(2)}, u32[]{:S(2)}) %collective-permute-start.1) | collective-permute-done | bytes 786464 | tf_op jit(solution)/shard_map/ppermute | solution.py:18
  114.1 2.2 %fusion = f32[4,512,512]{2,1,0:T(8,128)} fusion(f32[4,512,512]{2,1,0:T(8,128)} %slice.103, f32[4,96,512]{2,1,0:T(8,128)S(1)} %collective-permute-done.1, f32[4,608,512]{2,1,0:T(8,128)} %shard_map.82), kind=kLoop, calls=%fused_computation.2 | loop fusion | flops 196608 | bytes 2359296 | tf_op jit(solution)/shard_map/scatter-add | solution.py:147
  116.3 0.0 reduce-scatter.2.cloned.1.call-update
  116.3 61.5 %reduce-scatter.2.cloned.1.call-done = f32[4,32,512]{2,1,0:T(8,128)} async-done(((f32[4,512,512]{2,1,0:T(8,128)}), f32[4,32,512]{2,1,0:T(8,128)}) %reduce-scatter.2.cloned.1.call-update) | async-done | bytes 262160 | tf_op jit(solution)/shard_map/reduce_scatter | solution.py:148
  (2 shorter events, 0.0 us)
Async XLA Ops:
  6.5 50.8 %all-gather.2.cloned.1.call-start = ((), (), s32[]{:S(2)}) async-start(), calls=%async_computation.1 | async-start | bytes 2228224 | tf_op jit(solution)/shard_map/all_gather | solution.py:142
  7.3 170.5 %reduce-scatter.2.cloned.1.call-start = ((), (), s32[]{:S(2)}) async-start(), calls=%async_computation.2 | async-start | bytes 4456448 | tf_op jit(solution)/shard_map/reduce_scatter | solution.py:148
  58.4 13.5 %collective-permute-start = (bf16[4,96,512]{2,1,0:T(8,128)(2,1)S(1)}, bf16[4,96,512]{2,1,0:T(8,128)(2,1)S(1)}, u32[]{:S(2)}, u32[]{:S(2)}) collective-permute-start(bf16[4,96,512]{2,1,0:T(8,128)(2,1)S(1)} %slice.102), channel_id=1, source_target_pairs={{16,0},{32,16},{48,32},{64,48},{80,64},{96,80},{112,96},{128,112},... | collective-permute-start | bytes 1179656 | tf_op jit(solution)/shard_map/ppermute | solution.py:18
  87.5 26.6 %collective-permute-start.1 = (f32[4,96,512]{2,1,0:T(8,128)S(1)}, f32[4,96,512]{2,1,0:T(8,128)S(1)}, u32[]{:S(2)}, u32[]{:S(2)}) collective-permute-start(f32[4,96,512]{2,1,0:T(8,128)S(1)} %slice.105), channel_id=1, source_target_pairs={{0,16},{16,32},{32,48},{48,64},{64,80},{80,96},{96,112},{112,128},... | collective-permute-start | bytes 2359304 | tf_op jit(solution)/shard_map/ppermute | solution.py:18
Sparse Core Ops, SparseCore 0:
  9.5 47.8 all-gather.1
  116.4 61.3 reduce-scatter.1
